TPU v7x, 768 devices: a whole 4x8x12 slice. The times are simulated.
768 devices in a mesh: wide: 96 (over y, z), narrow: 8 (over x, core).
Axes of the slice: x: 4, y: 8, z: 12, core: 2. Of those that a mesh axis runs over, the one named last changes fastest.
Arguments:
- points: bfloat16 [3072, 256, 256], P('wide', 'narrow'), may hold values from -6 to 6
- targets: bfloat16 [3072, 256, 256], P('wide', 'narrow'), may hold values from -6 to 6
- centroids: float32 [1536, 256], P('wide'), may hold values from -3 to 3
- block_list: int32 [3072], P('wide'), may hold values from 0 to 15
- lengths: int32 [3072], P('wide'), may hold values from 1 to 256
- sources: int32 [3072], P('wide'), may hold values from 0 to 3071, as said below
Outputs:
- rotated: bfloat16 [3072, 256, 256], P('wide', 'narrow')
Inputs may be any that keep to these rules, and one draw needn't show every extreme that they name: For every index w of wide and slot j below 2, sources[w * 32 + j] = u * 32 + j for some index u of wide, each such input block named exactly once; every other entry names its own position.
All inputs are finite; a program needn't handle non-finite values.
Results may differ from a plain program's by a relative error of at most 0.0051.
Values may be sent and summed in bfloat16 or wider, within the bound.
A program may use at most 32 MiB of HBM per device.

v0:
```python
import jax
import jax.numpy as jnp
from jax import lax
from jax.sharding import PartitionSpec as P

MOVE = 2
ITERS = 5


highest_prec = lax.Precision.HIGHEST


def newton_polar(cross_gram):
    frob_norm = jnp.sqrt(jnp.sum(cross_gram * cross_gram, axis=(1, 2), keepdims=True) + 1e-06)
    polar_iter = cross_gram / frob_norm
    for sweep_index in range(ITERS):
        product = jnp.einsum("lde,lfe->ldf", polar_iter, polar_iter, precision=highest_prec)
        polar_iter = 1.5 * polar_iter - 0.5 * jnp.einsum(
            "ldf,lfe->lde", product, polar_iter, precision=highest_prec
        )
    return polar_iter.astype(jnp.bfloat16)


def local(points, targets, centroids, block_list, lengths, sources):
    block_count, rows_here, embed_width = points.shape
    list_count = centroids.shape[0]
    row_index = lax.axis_index("narrow") * rows_here + jnp.arange(rows_here, dtype=jnp.int32)
    in_range = row_index[None, :] < lengths[:, None]
    list_match = block_list[:, None] == jnp.arange(list_count, dtype=jnp.int32)[None, :]
    list_pick = list_match.astype(jnp.float32)
    centre_rows = jnp.dot(list_pick, centroids, precision=highest_prec)
    residual = jnp.where(
        in_range[:, :, None], points.astype(jnp.float32) - centre_rows[:, None, :], 0.0
    ).astype(jnp.bfloat16)
    block_grams = jnp.einsum("brd,bre->bde", residual, targets, preferred_element_type=jnp.float32)
    cross_gram = lax.psum_scatter(
        jnp.einsum("bl,bde->lde", list_pick, block_grams, precision=highest_prec),
        "narrow",
        scatter_dimension=0,
        tiled=True,
    )
    rotation = newton_polar(cross_gram)
    all_rotations = lax.all_gather(rotation, "narrow", axis=0, tiled=True)
    chosen = jnp.einsum(
        "bl,lde->bde",
        list_match.astype(jnp.bfloat16),
        all_rotations,
        preferred_element_type=jnp.float32,
    ).astype(jnp.bfloat16)
    turned = jnp.einsum(
        "brd,bde->bre", residual, chosen, preferred_element_type=jnp.float32
    ).astype(jnp.bfloat16)
    donor_index = sources[:MOVE] // block_count
    part_rows = lax.all_gather(turned[None, :MOVE], "wide", axis=0, tiled=True)
    how_many = part_rows.shape[0]
    selector = (donor_index[:, None] == jnp.arange(how_many, dtype=jnp.int32)[None, :]).astype(
        jnp.bfloat16
    )
    handed = jnp.einsum("ji,ijrd->jrd", selector, part_rows, preferred_element_type=jnp.float32)
    return jnp.concatenate([handed.astype(jnp.bfloat16), turned[MOVE:]], axis=0)


def solution(mesh):
    return jax.shard_map(
        local,
        mesh=mesh,
        in_specs=(
            P("wide", "narrow", None),
            P("wide", "narrow", None),
            P("wide", None),
            P("wide"),
            P("wide"),
            P("wide"),
        ),
        out_specs=P("wide", "narrow", None),
        check_vma=False,
    )
```

profile of v0, /device:TPU:24, one launch (start us, length us, event | category | flops | bytes accessed | tf_op | source)
XLA Modules:
  0.0 263.3 jit_solution(11894131143567300444)
XLA Ops:
  6.5 0.0 copy-start
  6.5 0.0 reduce-scatter.2.cloned.1.call-start
  6.5 1.0 fusion.17
  7.5 0.7 broadcast_compare_fusion
  8.3 0.0 copy-done
  8.3 0.0 copy-start.2
  8.3 3.4 %fusion.14 = f32[32,256,256]{2,1,0:T(8,128)S(1)} fusion(bf16[32,32,256]{2,1,0:T(8,128)(2,1)S(1)} %copy-done, bf16[32,32,256]{2,1,0:T(8,128)(2,1)} %param.6, f32[32,256]{1,0:T(8,128)S(1)} %fusion.17, pred[32,32]{1,0:T(8,128)(4,1)S(1)} %broadcast_compare_fusion), kind=kOutput, calls=%fused_computation.23 | convolution fusion | flops 135266304 | bytes 9470976 | tf_op jit(solution)/shard_map/brd,bre->bde/dot_general | solution.py:35
  11.7 0.0 copy-done.2
  11.7 8.1 %fusion = f32[16,256,256]{2,0,1:T(8,128)S(1)} fusion(f32[32,256,256]{2,1,0:T(8,128)S(1)} %fusion.14, s32[32]{0:T(128)S(1)} %copy-done.2), kind=kOutput, calls=%fused_computation.1 | convolution fusion | flops 402653696 | bytes 12583040 | tf_op jit(solution)/shard_map/bl,bde->lde/dot_general | solution.py:37
  19.8 4.6 %copy.15 = f32[16,256,256]{2,1,0:T(8,128)} copy(f32[16,256,256]{2,0,1:T(8,128)S(1)} %fusion) | data formatting | bytes 8388608 | tf_op jit(solution)/shard_map/bl,bde->lde/dot_general | solution.py:37
  24.4 0.0 reduce-scatter.2.cloned.1.call-update
  24.4 0.0 all-gather.4.cloned.1.call-start
  24.5 52.6 %reduce-scatter.2.cloned.1.call-done = f32[2,256,256]{2,1,0:T(8,128)} async-done(((f32[16,256,256]{2,1,0:T(8,128)}), f32[2,256,256]{2,1,0:T(8,128)}) %reduce-scatter.2.cloned.1.call-update) | async-done | bytes 524304 | tf_op jit(solution)/shard_map/reduce_scatter | solution.py:36
  77.1 1.2 multiply_reduce_fusion
  78.3 2.0 fusion.15
  80.2 2.0 fusion.12
  82.2 0.7 fusion.26
  82.9 0.7 fusion.11
  83.6 0.7 fusion.27
  84.2 0.7 fusion.10
  84.9 0.7 fusion.28
  85.6 0.7 fusion.9
  86.3 0.7 fusion.29
  87.0 0.0 copy-start.1
  87.0 1.4 fusion.13
  88.3 0.0 all-gather.4.cloned.1.call-update
  88.4 0.3 all-gather.6.cloned.1.call-start
  88.6 32.2 %all-gather.4.cloned.1.call-done = bf16[16,256,256]{2,1,0:T(8,128)(2,1)} async-done(((bf16[2,256,256]{2,1,0:T(8,128)(2,1)}), bf16[16,256,256]{2,1,0:T(8,128)(2,1)}) %all-gather.4.cloned.1.call-update) | async-done | bytes 2097168 | tf_op jit(solution)/shard_map/all_gather | solution.py:43
  120.9 3.1 %fusion.5 = bf16[32,256,256]{2,0,1:T(8,128)(2,1)S(1)} fusion(bf16[16,256,256]{2,1,0:T(8,128)(2,1)} %all-gather.4.cloned.1.call-done, s32[32]{0:T(128)S(1)} %copy-done.2), kind=kOutput, calls=%fused_computation.6 | convolution fusion | flops 67109376 | bytes 6291584 | tf_op jit(solution)/shard_map/bl,lde->bde/dot_general | solution.py:44
  124.0 0.0 copy-done.1
  124.0 0.0 copy-start.3
  124.0 2.4 fusion.7
  126.4 0.6 slice.12
  127.0 0.0 all-gather.6.cloned.1.call-update
  127.0 0.0 copy-done.3
  127.1 0.1 compare_bitcast_fusion
  127.2 125.1 %all-gather.6.cloned.1.call-done = bf16[192,32,256]{2,1,0:T(8,128)(2,1)} async-done(((bf16[2,32,256]{2,1,0:T(8,128)(2,1)}), bf16[192,32,256]{2,1,0:T(8,128)(2,1)}) %all-gather.6.cloned.1.call-update) | async-done | bytes 3145744 | tf_op jit(solution)/shard_map/all_gather | solution.py:54
  252.3 3.7 %fusion.3 = bf16[2,1,32,256]{3,1,2,0:T(2,128)(2,1)S(1)} fusion(bf16[96,2,32,256]{3,2,1,0:T(8,128)(2,1)} %bitcast.29, pred[2,96,1,1]{1,0,2,3:T(4,128)(4,1)S(1)} %compare_bitcast_fusion), kind=kOutput, calls=%fused_computation.4 | convolution fusion | flops 3145728 | bytes 3178688 | tf_op jit(solution)/shard_map/ji,ijrd->jrd/dot_general | solution.py:59
  256.0 0.8 pad_maximum_fusion
  (5 shorter events, 0.1 us)
Async XLA Ops:
  6.5 1.7 copy-start
  6.5 70.5 %reduce-scatter.2.cloned.1.call-start = ((), (), s32[]{:S(2)}) async-start(), calls=%async_computation.1 | async-start | bytes 4718592 | tf_op jit(solution)/shard_map/reduce_scatter | solution.py:36
  8.3 3.4 %copy-start.2 = (s32[32]{0:T(128)S(1)}, s32[32]{0:T(128)}, u32[]{:S(2)}) copy-start(s32[32]{0:T(128)} %param.9) | copy-start | bytes 388
  24.4 96.4 %all-gather.4.cloned.1.call-start = ((), (), s32[]{:S(2)}) async-start(), calls=%async_computation.2 | async-start | bytes 2359296 | tf_op jit(solution)/shard_map/all_gather | solution.py:43
  87.0 37.0 %copy-start.1 = (bf16[32,32,256]{2,1,0:T(8,128)(2,1)S(1)}, bf16[32,32,256]{2,1,0:T(8,128)(2,1)}, u32[]{:S(2)}) copy-start(bf16[32,32,256]{2,1,0:T(8,128)(2,1)} %param.6) | copy-start | bytes 1572868
  88.4 163.9 %all-gather.6.cloned.1.call-start = ((), (), s32[]{:S(2)}) async-start(), calls=%async_computation.3 | async-start | bytes 3178496 | tf_op jit(solution)/shard_map/all_gather | solution.py:54
  124.0 3.1 %copy-start.3 = (s32[32]{0:T(128)S(1)}, s32[32]{0:T(128)}, u32[]{:S(2)}) copy-start(s32[32]{0:T(128)} %param.11) | copy-start | bytes 388
Sparse Core Ops, SparseCore 0:
  24.5 52.4 reduce-scatter.1
  88.5 32.3 all-gather.3
  127.2 125.0 all-gather.5
where the time goes:
time: 264 us; the launch traced here: 263 us
  waiting for transfers between devices  210 us (80%)
  matrix products  31.7 us (12%)
  between operations  13.3 us (5%)
  local copies, waits for them, and re-layouts  5.23 us (2%)
  other arithmetic  2.87 us (1%)
    all_gather x1, waiting for transfers between devices, local(): part_rows = lax.all_gather(turned[None, :MOVE], 'wide', axis=0, tiled=True)  125 us
    reduce_scatter x1, waiting for transfers between devices, local(): lax.psum_scatter(jnp.einsum('bl,bde->lde', list_pick, block_grams, precis...  52.6 us
    all_gather x1, waiting for transfers between devices, local(): all_rotations = lax.all_gather(rotation, 'narrow', axis=0, tiled=True)  32.2 us
    dot_general x1, matrix products, local(): jnp.einsum('bl,bde->lde', list_pick, block_grams, precision=highest_prec)  8.11 us
    dot_general x5, matrix products, newton_polar(): jnp.einsum('ldf,lfe->lde', product, polar_iter, precision=highest_prec)  5.39 us
  transfers between devices with their start and end apart: 3, of which 3 were waited for; matrix products, arithmetic and copies ran while one was open for 0% of the time, Pallas kernels for 0%

commit v1 on v0

v1 whole, which is shorter than its diff:
```python
import functools

import jax
import jax.numpy as jnp
from jax import lax
from jax.experimental import pallas as pl
from jax.experimental.pallas import tpu as pltpu
from jax.sharding import PartitionSpec as P

MOVE = 2
SWEEPS = 5
CHIPS_X = 4
RING_Y = 8
RING_Z = 12
PER_DEV = 2

MESH = pl.DeviceIdType.MESH
BF16 = jnp.bfloat16
F32 = jnp.float32


def mm(a, b):
    return jnp.dot(a, b, preferred_element_type=F32)


def mm_nt(a, b):
    return lax.dot_general(a, b, (((1,), (1,)), ((), ())), preferred_element_type=F32)


def split_bf16(a):
    high = a.astype(BF16)
    return high, (a - high.astype(F32)).astype(BF16)


def remote(src, dst, send_sem, recv_sem, where):
    return pltpu.make_async_remote_copy(
        src_ref=src,
        dst_ref=dst,
        send_sem=send_sem,
        recv_sem=recv_sem,
        device_id=where,
        device_id_type=MESH,
    )


def x_partners(narrow):
    chip, core = narrow // 2, narrow % 2
    right = ((chip + 1) % CHIPS_X) * 2 + core
    left = ((chip + CHIPS_X - 1) % CHIPS_X) * 2 + core
    sibling = chip * 2 + 1 - core
    return chip, core, right, left, sibling


def reduce_kernel(
    blocks,
    rows,
    points,
    targets,
    centroids,
    block_list,
    lengths,
    gram_out,
    res_own,
    own_p,
    own_t,
    sib_p,
    sib_t,
    res_sib,
    turned_t,
    masked,
    kept,
    out_buf,
    in_buf,
    load_sem,
    send_sem,
    recv_sem,
):
    narrow = lax.axis_index("narrow")
    chip, core, right, left, sibling = x_partners(narrow)
    width = points.shape[1]
    total = blocks * rows

    load_t = pltpu.make_async_copy(targets, own_t, load_sem.at[0])
    load_p = pltpu.make_async_copy(points, own_p, load_sem.at[1])
    load_t.start()
    load_p.start()

    barrier = pltpu.get_barrier_semaphore()
    for partner in (sibling, right, left):
        pl.semaphore_signal(barrier, inc=1, device_id={"narrow": partner}, device_id_type=MESH)
    pl.semaphore_wait(barrier, 3)

    swap_t = remote(targets, sib_t, send_sem.at[6], recv_sem.at[6], {"narrow": sibling})
    swap_p = remote(points, sib_p, send_sem.at[7], recv_sem.at[7], {"narrow": sibling})
    swap_t.start()
    swap_p.start()

    def residual_into(dst, src, first_row):
        def one(b, carry):
            base = pl.multiple_of(b * rows, rows)
            centre = centroids[pl.ds(block_list[b], 1), :]
            row = first_row + lax.broadcasted_iota(jnp.int32, (rows, width), 0)
            value = src[pl.ds(base, rows), :].astype(F32) - centre
            dst[pl.ds(base, rows), :] = jnp.where(row < lengths[b], value, 0.0).astype(BF16)
            return carry

        lax.fori_loop(0, blocks, one, 0, unroll=4)

    def transpose_into(first, src):
        for piece in range(total // width):
            turned_t[:, first + piece * width : first + (piece + 1) * width] = src[
                piece * width : (piece + 1) * width, :
            ].T

    load_t.wait()
    transpose_into(0, own_t)
    load_p.wait()
    residual_into(res_own, own_p, narrow * rows)
    swap_t.wait_recv()
    transpose_into(total, sib_t)
    swap_p.wait_recv()
    residual_into(res_sib, sib_p, sibling * rows)

    def gram(owner_chip, which, slot):
        wanted = (owner_chip * 2 + core) * PER_DEV + which

        def one(b, carry):
            base = pl.multiple_of(b * rows, rows)
            keep = jnp.where(block_list[b] == wanted, 1.0, 0.0).astype(BF16)
            masked[slot, pl.ds(base, rows), :] = res_own[pl.ds(base, rows), :] * keep
            masked[slot, pl.ds(total + base, rows), :] = res_sib[pl.ds(base, rows), :] * keep
            return carry

        lax.fori_loop(0, blocks, one, 0, unroll=8)
        return mm(turned_t[...], masked[slot])

    opposite = (chip + 2) % CHIPS_X
    right_chip = (chip + 1) % CHIPS_X
    left_chip = (chip + CHIPS_X - 1) % CHIPS_X

    def hop(slot, where):
        return remote(
            out_buf.at[slot], in_buf.at[slot], send_sem.at[slot], recv_sem.at[slot], {"narrow": where}
        )

    hops = [hop(s, right if s % 2 == 0 else left) for s in range(6)]
    out_buf[0] = gram(opposite, 0, 0).astype(BF16)
    hops[0].start()
    out_buf[1] = gram(opposite, 1, 1).astype(BF16)
    hops[1].start()
    out_buf[2] = gram(right_chip, 1, 0).astype(BF16)
    hops[2].start()
    out_buf[3] = gram(left_chip, 0, 1).astype(BF16)
    hops[3].start()
    kept[0] = gram(right_chip, 0, 0)
    kept[1] = gram(left_chip, 1, 1)
    kept[2] = gram(chip, 0, 0)
    kept[3] = gram(chip, 1, 1)
    hops[0].wait_recv()
    out_buf[4] = (kept[0] + in_buf[0].astype(F32)).astype(BF16)
    hops[4].start()
    hops[1].wait_recv()
    out_buf[5] = (kept[1] + in_buf[1].astype(F32)).astype(BF16)
    hops[5].start()
    hops[3].wait_recv()
    kept[2] = kept[2] + in_buf[3].astype(F32)
    hops[2].wait_recv()
    kept[3] = kept[3] + in_buf[2].astype(F32)
    hops[4].wait_recv()
    gram_out[0] = kept[2] + in_buf[4].astype(F32)
    hops[5].wait_recv()
    gram_out[1] = kept[3] + in_buf[5].astype(F32)
    for copy in hops:
        copy.wait_send()
    swap_t.wait_send()
    swap_p.wait_send()


def turn_kernel(
    blocks,
    rows,
    gram_in,
    res,
    block_list,
    sources,
    out,
    iterate,
    rot,
    hand0,
    hand1,
    got_z,
    got_y,
    pass_y,
    pass_z,
    last_y,
    last_z,
    ask,
    ask_y,
    ask_z,
    read_y,
    read_z,
    rot_send,
    rot_recv,
    ask_sy,
    ask_sz,
    ask_ry,
    ask_rz,
    g_sz,
    g_rz,
    g_sy,
    g_ry,
    p_sy,
    p_ry,
    p_sz,
    p_rz,
    read_sem,
):
    wide = lax.axis_index("wide")
    narrow = lax.axis_index("narrow")
    at_y, at_z = wide // RING_Z, wide % RING_Z
    chip, core, right, left, sibling = x_partners(narrow)

    def y_peer(step):
        other = (at_y + step) % RING_Y
        return other, {"wide": other * RING_Z + at_z}

    def z_peer(step):
        other = (at_z + step) % RING_Z
        return other, {"wide": at_y * RING_Z + other}

    y_steps = sorted(range(1, RING_Y), key=lambda s: -min(s, RING_Y - s))
    z_steps = sorted(range(1, RING_Z), key=lambda s: -min(s, RING_Z - s))

    barrier = pltpu.get_barrier_semaphore()
    for step in z_steps:
        pl.semaphore_signal(barrier, inc=1, device_id=z_peer(step)[1], device_id_type=MESH)
    for step in y_steps:
        pl.semaphore_signal(barrier, inc=1, device_id=y_peer(step)[1], device_id_type=MESH)
    for partner in (sibling, right, left):
        pl.semaphore_signal(barrier, inc=1, device_id={"narrow": partner}, device_id_type=MESH)

    line = lax.broadcasted_iota(jnp.int32, ask.shape, 0)
    ask[...] = jnp.where(line == 0, sources[0], sources[1])
    ask_y[at_y] = ask[...]
    ask_z[at_z] = ask[...]

    for which in range(PER_DEV):
        gram = gram_in[which]
        norm = jnp.sqrt(jnp.sum(gram * gram, keepdims=True) + 1e-06)
        iterate[which] = gram / norm

    def sweep(index, carry):
        for which in range(PER_DEV):
            held = iterate[which].astype(BF16)
            product = mm_nt(held, held).astype(BF16)
            iterate[which] = 1.5 * iterate[which] - 0.5 * mm(product, held)
        return carry

    lax.fori_loop(0, SWEEPS - 1, sweep, 0)
    for which in range(PER_DEV):
        exact = iterate[which]
        high, low = split_bf16(exact)
        product = mm_nt(high, high) + (mm_nt(high, low) + mm_nt(low, high))
        p_high, p_low = split_bf16(product)
        cubed = mm(p_high, high) + (mm(p_high, low) + mm(p_low, high))
        rot[narrow * PER_DEV + which] = (1.5 * exact - 0.5 * cubed).astype(BF16)

    pl.semaphore_wait(barrier, RING_Y - 1 + RING_Z - 1 + 3)

    right_chip = (chip + 1) % CHIPS_X
    left_chip = (chip + CHIPS_X - 1) % CHIPS_X
    opposite = (chip + 2) % CHIPS_X

    def place(owner_chip, owner_core, which):
        return (owner_chip * 2 + owner_core) * PER_DEV + which

    sent = []

    def share(slot, where):
        copy = remote(
            rot.at[slot], rot.at[slot], rot_send.at[len(sent)], rot_recv.at[slot], {"narrow": where}
        )
        copy.start()
        sent.append(copy)

    def arrived(slot):
        remote(rot.at[slot], rot.at[slot], rot_send.at[0], rot_recv.at[slot], {"narrow": sibling}).wait_recv()

    share(place(chip, core, 0), right)
    share(place(chip, core, 1), left)
    share(place(chip, core, 1), right)
    share(place(chip, core, 0), left)
    share(place(chip, core, 0), sibling)
    share(place(chip, core, 1), sibling)

    asks = []
    for step in y_steps:
        other, where = y_peer(step)
        copy = remote(ask, ask_y.at[at_y], ask_sy.at[step], ask_ry.at[at_y], where)
        copy.start()
        asks.append(copy)
    for step in z_steps:
        other, where = z_peer(step)
        copy = remote(ask, ask_z.at[at_z], ask_sz.at[step], ask_rz.at[at_z], where)
        copy.start()
        asks.append(copy)

    arrived(place(left_chip, core, 0))
    share(place(left_chip, core, 0), right)
    share(place(left_chip, core, 0), sibling)
    arrived(place(right_chip, core, 1))
    share(place(right_chip, core, 1), left)
    share(place(right_chip, core, 1), sibling)
    arrived(place(left_chip, core, 1))
    share(place(left_chip, core, 1), sibling)
    arrived(place(right_chip, core, 0))
    share(place(right_chip, core, 0), sibling)

    for step in y_steps:
        other, where = y_peer(step)
        remote(ask, ask_y.at[other], ask_sy.at[step], ask_ry.at[other], where).wait_recv()
    for step in z_steps:
        other, where = z_peer(step)
        remote(ask, ask_z.at[other], ask_sz.at[step], ask_rz.at[other], where).wait_recv()
    to_scalars_y = pltpu.make_async_copy(ask_y, read_y, read_sem.at[0])
    to_scalars_z = pltpu.make_async_copy(ask_z, read_z, read_sem.at[1])
    to_scalars_y.start()
    to_scalars_z.start()
    to_scalars_y.wait()
    to_scalars_z.wait()

    arrived(place(opposite, core, 0))
    share(place(opposite, core, 0), sibling)
    arrived(place(opposite, core, 1))
    share(place(opposite, core, 1), sibling)
    for owner_chip in (chip, left_chip, right_chip, opposite):
        for which in range(PER_DEV):
            arrived(place(owner_chip, 1 - core, which))

    def turn(b):
        base = pl.multiple_of(b * rows, rows)
        return mm_nt(res[pl.ds(base, rows), :], rot[block_list[b]]).astype(BF16)

    first, second = turn(0), turn(1)
    hand0[...] = first
    hand1[...] = second
    got_z[at_z] = first
    got_y[at_y] = second
    moves = []
    for step in z_steps:
        other, where = z_peer(step)
        copy = remote(hand0, got_z.at[at_z], g_sz.at[step], g_rz.at[at_z], where)
        copy.start()
        moves.append(copy)
    for step in y_steps:
        other, where = y_peer(step)
        copy = remote(hand1, got_y.at[at_y], g_sy.at[step], g_ry.at[at_y], where)
        copy.start()
        moves.append(copy)

    def turn_one(b, carry):
        out[pl.ds(pl.multiple_of(b * rows, rows), rows), :] = turn(b)
        return carry

    lax.fori_loop(MOVE, blocks, turn_one, 0, unroll=2)

    def from_y(source):
        return source // blocks // RING_Z

    def from_z(source):
        return source // blocks % RING_Z

    for step in y_steps:
        other, where = y_peer(step)
        remote(hand1, got_y.at[other], g_sy.at[step], g_ry.at[other], where).wait_recv()
    last_z[at_z] = got_y[from_y(sources[1])]
    for step in z_steps:
        other, where = z_peer(step)
        pass_z[other] = got_y[from_y(read_z[other, 1, 0])]
        copy = remote(pass_z.at[other], last_z.at[at_z], p_sz.at[step], p_rz.at[at_z], where)
        copy.start()
        moves.append(copy)

    for step in z_steps:
        other, where = z_peer(step)
        remote(hand0, got_z.at[other], g_sz.at[step], g_rz.at[other], where).wait_recv()
    last_y[at_y] = got_z[from_z(sources[0])]
    for step in y_steps:
        other, where = y_peer(step)
        pass_y[other] = got_z[from_z(read_y[other, 0, 0])]
        copy = remote(pass_y.at[other], last_y.at[at_y], p_sy.at[step], p_ry.at[at_y], where)
        copy.start()
        moves.append(copy)

    for step in y_steps:
        other, where = y_peer(step)
        remote(hand1, last_y.at[other], p_sy.at[step], p_ry.at[other], where).wait_recv()
    out[0:rows, :] = last_y[from_y(sources[0])]
    for step in z_steps:
        other, where = z_peer(step)
        remote(hand0, last_z.at[other], p_sz.at[step], p_rz.at[other], where).wait_recv()
    out[rows : 2 * rows, :] = last_z[from_z(sources[1])]

    for copy in sent + asks + moves:
        copy.wait_send()


def local(points, targets, centroids, block_list, lengths, sources):
    blocks, rows, width = points.shape
    lists = centroids.shape[0]
    total = blocks * rows
    vmem = pl.BlockSpec(memory_space=pltpu.VMEM)
    smem = pl.BlockSpec(memory_space=pltpu.SMEM)
    anywhere = pl.BlockSpec(memory_space=pl.ANY)
    dma = pltpu.SemaphoreType.DMA
    square = (width, width)
    gram, residual = pl.pallas_call(
        functools.partial(reduce_kernel, blocks, rows),
        out_shape=(
            jax.ShapeDtypeStruct((PER_DEV, *square), F32),
            jax.ShapeDtypeStruct((total, width), BF16),
        ),
        in_specs=[anywhere, anywhere, vmem, smem, smem],
        out_specs=(vmem, vmem),
        scratch_shapes=[
            pltpu.VMEM((total, width), BF16),
            pltpu.VMEM((total, width), BF16),
            pltpu.VMEM((total, width), BF16),
            pltpu.VMEM((total, width), BF16),
            pltpu.VMEM((total, width), BF16),
            pltpu.VMEM((width, 2 * total), BF16),
            pltpu.VMEM((2, 2 * total, width), BF16),
            pltpu.VMEM((4, *square), F32),
            pltpu.VMEM((6, *square), BF16),
            pltpu.VMEM((6, *square), BF16),
            dma((2,)),
            dma((8,)),
            dma((8,)),
        ],
        compiler_params=pltpu.CompilerParams(collective_id=0, has_side_effects=True),
        name="reduce_grams",
    )(
        points.reshape(total, width),
        targets.reshape(total, width),
        centroids,
        block_list,
        lengths,
    )
    tile = (rows, width)
    ask = (8, 128)
    rotated = pl.pallas_call(
        functools.partial(turn_kernel, blocks, rows),
        out_shape=jax.ShapeDtypeStruct((total, width), BF16),
        in_specs=[vmem, vmem, smem, smem],
        out_specs=vmem,
        scratch_shapes=[
            pltpu.VMEM((PER_DEV, *square), F32),
            pltpu.VMEM((lists, *square), BF16),
            pltpu.VMEM(tile, BF16),
            pltpu.VMEM(tile, BF16),
            pltpu.VMEM((RING_Z, *tile), BF16),
            pltpu.VMEM((RING_Y, *tile), BF16),
            pltpu.VMEM((RING_Y, *tile), BF16),
            pltpu.VMEM((RING_Z, *tile), BF16),
            pltpu.VMEM((RING_Y, *tile), BF16),
            pltpu.VMEM((RING_Z, *tile), BF16),
            pltpu.VMEM(ask, jnp.int32),
            pltpu.VMEM((RING_Y, *ask), jnp.int32),
            pltpu.VMEM((RING_Z, *ask), jnp.int32),
            pltpu.SMEM((RING_Y, *ask), jnp.int32),
            pltpu.SMEM((RING_Z, *ask), jnp.int32),
            dma((14,)),
            dma((lists,)),
            dma((RING_Y,)),
            dma((RING_Z,)),
            dma((RING_Y,)),
            dma((RING_Z,)),
            dma((RING_Z,)),
            dma((RING_Z,)),
            dma((RING_Y,)),
            dma((RING_Y,)),
            dma((RING_Y,)),
            dma((RING_Y,)),
            dma((RING_Z,)),
            dma((RING_Z,)),
            dma((2,)),
        ],
        compiler_params=pltpu.CompilerParams(collective_id=1, has_side_effects=True),
        name="turn_and_hand",
    )(gram, residual, block_list, sources)
    return rotated.reshape(blocks, rows, width)


def solution(mesh):
    return jax.shard_map(
        local,
        mesh=mesh,
        in_specs=(
            P("wide", "narrow", None),
            P("wide", "narrow", None),
            P("wide", None),
            P("wide"),
            P("wide"),
            P("wide"),
        ),
        out_specs=P("wide", "narrow", None),
        check_vma=False,
    )
```

time: 264 us -> 72.5 us (0.27)
  the two profiles are of different devices: /device:TPU:24 before, /device:TPU:1 now
where the time goes in v1:
time: 72.5 us; the launch traced here: 72.2 us
  Pallas kernels  70.3 us (97%)
  local copies, waits for them, and re-layouts  1.87 us (3%)
    pallas_call x1, Pallas kernels, local(): pl.pallas_call(functools.partial(turn_kernel, blocks, rows), out_shape=ja...  41.7 us
    pallas_call x1, Pallas kernels, local(): pl.pallas_call(functools.partial(reduce_kernel, blocks, rows), out_shape=...  28.5 us
    unnamed x1, local copies, waits for them, and re-layouts  1.87 us

profile of v1, /device:TPU:1, one launch (start us, length us, event | category | flops | bytes accessed | tf_op | source)
XLA Modules:
  0.0 72.2 jit_solution(8199389271056377917)
XLA Ops:
  0.0 28.5 %reduce_grams.1 = (f32[2,256,256]{2,1,0:T(8,128)}, bf16[1024,256]{1,0:T(8,128)(2,1)}) custom-call(bf16[1024,256]{1,0:T(8,128)(2,1)} %bitcast.4, bf16[1024,256]{1,0:T(8,128)(2,1)} %bitcast.5, f32[16,256]{1,0:T(8,128)} %centroids.1, s32[32]{0:T(128)} %block_list.3, s32[32]{0:T(128)} %lengths.1), custom_call_target="tpu_custom_call" | custom-call | tf_op jit(solution)/shard_map/reduce_grams/pallas_call | solution.py:417
  28.6 41.7 %turn_and_hand.1 = bf16[1024,256]{1,0:T(8,128)(2,1)} custom-call(f32[2,256,256]{2,1,0:T(8,128)} %get-tuple-element.7.gram_in, bf16[1024,256]{1,0:T(8,128)(2,1)} %get-tuple-element.8.res, s32[32]{0:T(128)} %block_list.3, s32[32]{0:T(128)} %sources.1), custom_call_target="tpu_custom_call" | custom-call | tf_op jit(solution)/shard_map/turn_and_hand/pallas_call | solution.py:451
  70.3 1.9 %copy.8 = bf16[32,32,256]{2,1,0:T(8,128)(2,1)} copy(bf16[32,32,256]{2,1,0:T(8,128)(2,1)} %bitcast.3) | data formatting | bytes 1048576

commit v2 on v1

v2 whole, which is shorter than its diff:
```python
import functools

import jax
import jax.numpy as jnp
from jax import lax
from jax.experimental import pallas as pl
from jax.experimental.pallas import tpu as pltpu
from jax.sharding import PartitionSpec as P

MOVE = 2
SWEEPS = 5
CHIPS_X = 4
RING_Y = 8
RING_Z = 12
PER_DEV = 2

MESH = pl.DeviceIdType.MESH
BF16 = jnp.bfloat16
F32 = jnp.float32


def mm(a, b):
    return jnp.dot(a, b, preferred_element_type=F32)


def mm_nt(a, b):
    return lax.dot_general(a, b, (((1,), (1,)), ((), ())), preferred_element_type=F32)


def split_bf16(a):
    high = a.astype(BF16)
    return high, (a - high.astype(F32)).astype(BF16)


def remote(src, dst, send_sem, recv_sem, where):
    return pltpu.make_async_remote_copy(
        src_ref=src,
        dst_ref=dst,
        send_sem=send_sem,
        recv_sem=recv_sem,
        device_id=where,
        device_id_type=MESH,
    )


def x_partners(narrow):
    chip, core = narrow // 2, narrow % 2
    right = ((chip + 1) % CHIPS_X) * 2 + core
    left = ((chip + CHIPS_X - 1) % CHIPS_X) * 2 + core
    sibling = chip * 2 + 1 - core
    return chip, core, right, left, sibling


def kernel(
    blocks,
    rows,
    points,
    targets,
    centroids_hbm,
    block_list_hbm,
    lengths_hbm,
    sources_hbm,
    out,
    centroids,
    block_list,
    lengths,
    sources,
    own_p,
    own_t,
    sib_p,
    sib_t,
    res,
    res_sib,
    turned_t,
    kept,
    out_buf,
    in_buf,
    raw,
    hand_res,
    iterate,
    mine,
    rot,
    swap_out,
    swap_in,
    hand0,
    hand1,
    got_z,
    got_y,
    pass_y,
    pass_z,
    last_y,
    last_z,
    ask,
    ask_y,
    ask_z,
    read_y,
    read_z,
    load_sem,
    swap_send,
    swap_recv,
    raw_send,
    raw_recv,
    gram_send,
    gram_recv,
    x_send,
    x_recv,
    rot_send,
    rot_recv,
    ask_sy,
    ask_sz,
    ask_ry,
    ask_rz,
    g_sz,
    g_rz,
    g_sy,
    g_ry,
    p_sy,
    p_ry,
    p_sz,
    p_rz,
    read_sem,
    near_sem,
):
    wide = lax.axis_index("wide")
    narrow = lax.axis_index("narrow")
    at_y, at_z = wide // RING_Z, wide % RING_Z
    chip, core, right, left, sibling = x_partners(narrow)
    right_chip = (chip + 1) % CHIPS_X
    left_chip = (chip + CHIPS_X - 1) % CHIPS_X
    opposite = (chip + 2) % CHIPS_X
    width = points.shape[1]
    total = blocks * rows
    handed = MOVE * rows

    def y_peer(step):
        other = (at_y + step) % RING_Y
        return other, {"wide": other * RING_Z + at_z}

    def z_peer(step):
        other = (at_z + step) % RING_Z
        return other, {"wide": at_y * RING_Z + other}

    y_steps = sorted(range(1, RING_Y), key=lambda s: -min(s, RING_Y - s))
    z_steps = sorted(range(1, RING_Z), key=lambda s: -min(s, RING_Z - s))
    around = (
        y_peer(1)[1],
        y_peer(RING_Y - 1)[1],
        z_peer(1)[1],
        z_peer(RING_Z - 1)[1],
    )

    barrier = pltpu.get_barrier_semaphore()
    for partner in (sibling, right, left):
        pl.semaphore_signal(barrier, inc=1, device_id={"narrow": partner}, device_id_type=MESH)
    for where in around:
        pl.semaphore_signal(barrier, inc=1, device_id=where, device_id_type=MESH)

    loads = [
        pltpu.make_async_copy(source, target, load_sem.at[index])
        for index, (source, target) in enumerate(
            (
                (targets, own_t),
                (points, own_p),
                (block_list_hbm, block_list),
                (lengths_hbm, lengths),
                (centroids_hbm, centroids),
                (sources_hbm, sources),
            )
        )
    ]
    for load in loads:
        load.start()
    pl.semaphore_wait(barrier, 3 + len(around))

    swap_t = remote(targets, sib_t, swap_send.at[0], swap_recv.at[0], {"narrow": sibling})
    swap_p = remote(points, sib_p, swap_send.at[1], swap_recv.at[1], {"narrow": sibling})
    swap_t.start()
    swap_p.start()
    sent = [swap_t, swap_p]

    raws = []

    def share_raw(src, owner, where):
        copy = remote(src, raw.at[owner], raw_send.at[len(raws)], raw_recv.at[owner], {"narrow": where})
        copy.start()
        raws.append(copy)

    def raw_arrived(owner):
        remote(
            raw.at[owner], raw.at[owner], raw_send.at[0], raw_recv.at[owner], {"narrow": sibling}
        ).wait_recv()

    share_raw(points.at[pl.ds(0, handed)], narrow, right)
    share_raw(points.at[pl.ds(0, handed)], narrow, left)

    def tell():
        for index, where in enumerate(around):
            pl.semaphore_signal(near_sem.at[index], inc=1, device_id=where, device_id_type=MESH)

    def tell_z():
        for index in (2, 3):
            pl.semaphore_signal(near_sem.at[index], inc=1, device_id=around[index], device_id_type=MESH)

    def hear(kinds):
        for index in kinds:
            pl.semaphore_wait(near_sem.at[index], 1)

    tell()

    def residual_of(value, block, first_row):
        centre = centroids[pl.ds(block_list[block], 1), :]
        row = first_row + lax.broadcasted_iota(jnp.int32, (rows, width), 0)
        return jnp.where(row < lengths[block], value.astype(F32) - centre, 0.0).astype(BF16)

    def residual_into(dst, src, first_row):
        def one(b, carry):
            here = pl.ds(pl.multiple_of(b * rows, rows), rows)
            dst[here, :] = residual_of(src[here, :], b, first_row)
            return carry

        lax.fori_loop(0, blocks, one, 0, unroll=4)

    def transpose_into(first, src):
        for piece in range(total // width):
            turned_t[:, first + piece * width : first + (piece + 1) * width] = src[
                piece * width : (piece + 1) * width, :
            ].T

    loads[0].wait()
    transpose_into(0, own_t)
    for load in loads[1:]:
        load.wait()
    residual_into(res, own_p, narrow * rows)
    swap_t.wait_recv()
    transpose_into(total, sib_t)
    swap_p.wait_recv()
    raw_arrived(left)
    share_raw(raw.at[left], left, right)
    residual_into(res_sib, sib_p, sibling * rows)

    def gram(owner_chip, which):
        wanted = (owner_chip * 2 + core) * PER_DEV + which
        pieces = []
        for held in (res, res_sib):
            for b in range(blocks):
                keep = jnp.where(block_list[b] == wanted, 1.0, 0.0).astype(BF16)
                pieces.append(held[b * rows : (b + 1) * rows, :] * keep)
        return mm(turned_t[...], jnp.concatenate(pieces, axis=0))

    def hop(slot, where):
        return remote(
            out_buf.at[slot], in_buf.at[slot], gram_send.at[slot], gram_recv.at[slot], {"narrow": where}
        )

    hops = [hop(s, right if s % 2 == 0 else left) for s in range(6)]
    sent += hops
    out_buf[0] = gram(opposite, 0).astype(BF16)
    hops[0].start()
    out_buf[1] = gram(opposite, 1).astype(BF16)
    hops[1].start()
    hear((0, 1, 2, 3))
    tell()
    out_buf[2] = gram(right_chip, 1).astype(BF16)
    hops[2].start()
    share_raw(raw.at[left], left, sibling)
    raw_arrived(right)
    share_raw(raw.at[right], right, sibling)
    out_buf[3] = gram(left_chip, 0).astype(BF16)
    hops[3].start()
    hear((0, 1, 2, 3))
    tell()
    kept[0] = gram(right_chip, 0)
    kept[1] = gram(left_chip, 1)
    hear((0, 1, 2, 3))
    tell_z()
    across = opposite * 2 + core
    raw_arrived(across)
    share_raw(raw.at[across], across, sibling)
    kept[2] = gram(chip, 0)
    hear((2, 3))
    tell_z()
    kept[3] = gram(chip, 1)
    hear((2, 3))

    line = lax.broadcasted_iota(jnp.int32, ask.shape, 0)
    wish = jnp.where(line == 0, sources[0], sources[1])
    ask[...] = wish
    ask_y[at_y] = wish
    ask_z[at_z] = wish

    hops[0].wait_recv()
    out_buf[4] = (kept[0] + in_buf[0].astype(F32)).astype(BF16)
    hops[4].start()
    hops[1].wait_recv()
    out_buf[5] = (kept[1] + in_buf[1].astype(F32)).astype(BF16)
    hops[5].start()

    for step in y_steps:
        other, where = y_peer(step)
        copy = remote(ask, ask_y.at[at_y], ask_sy.at[step], ask_ry.at[at_y], where)
        copy.start()
        sent.append(copy)
    for step in z_steps:
        other, where = z_peer(step)
        copy = remote(ask, ask_z.at[at_z], ask_sz.at[step], ask_rz.at[at_z], where)
        copy.start()
        sent.append(copy)

    for b in range(MOVE):
        hand_res[b, pl.ds(pl.multiple_of(narrow * rows, rows), rows), :] = res[
            b * rows : (b + 1) * rows, :
        ]
        hand_res[b, pl.ds(pl.multiple_of(sibling * rows, rows), rows), :] = res_sib[
            b * rows : (b + 1) * rows, :
        ]
    for owner_chip in (left_chip, right_chip, opposite):
        raw_arrived(owner_chip * 2 + 1 - core)
        for owner_core in range(2):
            owner = owner_chip * 2 + owner_core
            for b in range(MOVE):
                hand_res[b, pl.ds(pl.multiple_of(owner * rows, rows), rows), :] = residual_of(
                    raw[owner, b * rows : (b + 1) * rows, :], b, owner * rows
                )

    hops[3].wait_recv()
    kept[2] = kept[2] + in_buf[3].astype(F32)
    hops[2].wait_recv()
    kept[3] = kept[3] + in_buf[2].astype(F32)
    hops[4].wait_recv()
    hops[5].wait_recv()
    for which in range(PER_DEV):
        total_gram = kept[2 + which] + in_buf[4 + which].astype(F32)
        norm = jnp.sqrt(jnp.sum(total_gram * total_gram, keepdims=True) + 1e-06)
        iterate[which] = total_gram / norm

    def sweep(index, carry):
        for which in range(PER_DEV):
            held = iterate[which].astype(BF16)
            product = mm_nt(held, held).astype(BF16)
            iterate[which] = 1.5 * iterate[which] - 0.5 * mm(product, held)
        return carry

    lax.fori_loop(0, SWEEPS - 1, sweep, 0)
    for which in range(PER_DEV):
        exact = iterate[which]
        high, low = split_bf16(exact)
        product = mm_nt(high, high) + (mm_nt(high, low) + mm_nt(low, high))
        p_high, p_low = split_bf16(product)
        cubed = mm(p_high, high) + (mm(p_high, low) + mm(p_low, high))
        rotation = (1.5 * exact - 0.5 * cubed).astype(BF16)
        mine[which] = rotation
        rot[narrow * PER_DEV + which] = rotation

    x_moves = []
    for b in range(MOVE):
        chosen = mine[block_list[b] % PER_DEV]
        swap_out[:, b * rows : (b + 1) * rows, :] = (
            mm_nt(hand_res[b], chosen).astype(BF16).reshape(2 * CHIPS_X, rows, width)
        )
    swap_in[narrow] = swap_out[narrow]
    for chip_step, flip in ((2, 0), (2, 1), (1, 0), (1, 1), (3, 0), (3, 1), (0, 1)):
        peer_core = core + flip - 2 * core * flip
        peer = ((chip + chip_step) % CHIPS_X) * 2 + peer_core
        copy = remote(
            swap_out.at[peer], swap_in.at[narrow], x_send.at[peer], x_recv.at[narrow], {"narrow": peer}
        )
        copy.start()
        x_moves.append((copy, peer))
    sent += [copy for copy, peer in x_moves]

    def place(owner_chip, owner_core, which):
        return (owner_chip * 2 + owner_core) * PER_DEV + which

    shares = []

    def share(slot, where):
        copy = remote(
            rot.at[slot], rot.at[slot], rot_send.at[len(shares)], rot_recv.at[slot], {"narrow": where}
        )
        copy.start()
        shares.append(copy)

    def arrived(slot):
        remote(rot.at[slot], rot.at[slot], rot_send.at[0], rot_recv.at[slot], {"narrow": sibling}).wait_recv()

    share(place(chip, core, 0), right)
    share(place(chip, core, 1), left)
    share(place(chip, core, 1), right)
    share(place(chip, core, 0), left)
    share(place(chip, core, 0), sibling)
    share(place(chip, core, 1), sibling)

    for step in y_steps:
        other, where = y_peer(step)
        remote(ask, ask_y.at[other], ask_sy.at[step], ask_ry.at[other], where).wait_recv()
    for step in z_steps:
        other, where = z_peer(step)
        remote(ask, ask_z.at[other], ask_sz.at[step], ask_rz.at[other], where).wait_recv()
    to_scalars_y = pltpu.make_async_copy(ask_y, read_y, read_sem.at[0])
    to_scalars_z = pltpu.make_async_copy(ask_z, read_z, read_sem.at[1])
    to_scalars_y.start()
    to_scalars_z.start()
    to_scalars_y.wait()
    to_scalars_z.wait()

    for copy, peer in x_moves:
        remote(
            swap_out.at[peer], swap_in.at[peer], x_send.at[peer], x_recv.at[peer], {"narrow": peer}
        ).wait_recv()
    first = swap_in[block_list[0] // PER_DEV][0:rows, :]
    second = swap_in[block_list[1] // PER_DEV][rows : 2 * rows, :]
    hand0[...] = first
    hand1[...] = second
    got_z[at_z] = first
    got_y[at_y] = second
    for step in y_steps:
        other, where = y_peer(step)
        copy = remote(hand1, got_y.at[at_y], g_sy.at[step], g_ry.at[at_y], where)
        copy.start()
        sent.append(copy)
    for step in z_steps:
        other, where = z_peer(step)
        copy = remote(hand0, got_z.at[at_z], g_sz.at[step], g_rz.at[at_z], where)
        copy.start()
        sent.append(copy)

    def turn(b):
        base = pl.multiple_of(b * rows, rows)
        return mm_nt(res[pl.ds(base, rows), :], rot[block_list[b]]).astype(BF16)

    def from_y(source):
        return source // blocks // RING_Z

    def from_z(source):
        return source // blocks % RING_Z

    arrived(place(right_chip, core, 1))
    share(place(right_chip, core, 1), left)
    share(place(right_chip, core, 1), sibling)
    arrived(place(left_chip, core, 0))
    share(place(left_chip, core, 0), right)
    share(place(left_chip, core, 0), sibling)

    for step in y_steps:
        other, where = y_peer(step)
        remote(hand1, got_y.at[other], g_sy.at[step], g_ry.at[other], where).wait_recv()
    last_z[at_z] = got_y[from_y(sources[1])]
    for step in z_steps:
        other, where = z_peer(step)
        pass_z[other] = got_y[from_y(read_z[other, 1, 0])]
        copy = remote(pass_z.at[other], last_z.at[at_z], p_sz.at[step], p_rz.at[at_z], where)
        copy.start()
        sent.append(copy)

    arrived(place(right_chip, core, 0))
    share(place(right_chip, core, 0), sibling)
    arrived(place(left_chip, core, 1))
    share(place(left_chip, core, 1), sibling)

    for step in z_steps:
        other, where = z_peer(step)
        remote(hand0, got_z.at[other], g_sz.at[step], g_rz.at[other], where).wait_recv()
    last_y[at_y] = got_z[from_z(sources[0])]
    for step in y_steps:
        other, where = y_peer(step)
        pass_y[other] = got_z[from_z(read_y[other, 0, 0])]
        copy = remote(pass_y.at[other], last_y.at[at_y], p_sy.at[step], p_ry.at[at_y], where)
        copy.start()
        sent.append(copy)

    arrived(place(opposite, core, 1))
    share(place(opposite, core, 1), sibling)
    arrived(place(opposite, core, 0))
    share(place(opposite, core, 0), sibling)
    for owner_chip in (chip, left_chip, right_chip, opposite):
        for which in range(PER_DEV):
            arrived(place(owner_chip, 1 - core, which))

    def turn_one(b, carry):
        out[pl.ds(pl.multiple_of(b * rows, rows), rows), :] = turn(b)
        return carry

    lax.fori_loop(MOVE, blocks, turn_one, 0, unroll=2)

    for step in y_steps:
        other, where = y_peer(step)
        remote(hand1, last_y.at[other], p_sy.at[step], p_ry.at[other], where).wait_recv()
    out[0:rows, :] = last_y[from_y(sources[0])]
    for step in z_steps:
        other, where = z_peer(step)
        remote(hand0, last_z.at[other], p_sz.at[step], p_rz.at[other], where).wait_recv()
    out[rows : 2 * rows, :] = last_z[from_z(sources[1])]

    for copy in sent + raws + shares:
        copy.wait_send()


def local(points, targets, centroids, block_list, lengths, sources):
    blocks, rows, width = points.shape
    lists = centroids.shape[0]
    total = blocks * rows
    narrow_size = 2 * CHIPS_X
    hbm = pl.BlockSpec(memory_space=pltpu.HBM)
    dma = pltpu.SemaphoreType.DMA
    square = (width, width)
    tile = (rows, width)
    ask = (8, 128)
    rotated = pl.pallas_call(
        functools.partial(kernel, blocks, rows),
        out_shape=jax.ShapeDtypeStruct((total, width), BF16),
        in_specs=[hbm] * 6,
        out_specs=pl.BlockSpec(memory_space=pltpu.VMEM),
        scratch_shapes=[
            pltpu.VMEM(centroids.shape, F32),
            pltpu.SMEM((blocks,), jnp.int32),
            pltpu.SMEM((blocks,), jnp.int32),
            pltpu.SMEM((blocks,), jnp.int32),
            *[pltpu.VMEM((total, width), BF16)] * 6,
            pltpu.VMEM((width, 2 * total), BF16),
            pltpu.VMEM((4, *square), F32),
            pltpu.VMEM((6, *square), BF16),
            pltpu.VMEM((6, *square), BF16),
            pltpu.VMEM((narrow_size, MOVE * rows, width), BF16),
            pltpu.VMEM((MOVE, narrow_size * rows, width), BF16),
            pltpu.VMEM((PER_DEV, *square), F32),
            pltpu.VMEM((PER_DEV, *square), BF16),
            pltpu.VMEM((lists, *square), BF16),
            pltpu.VMEM((narrow_size, MOVE * rows, width), BF16),
            pltpu.VMEM((narrow_size, MOVE * rows, width), BF16),
            pltpu.VMEM(tile, BF16),
            pltpu.VMEM(tile, BF16),
            pltpu.VMEM((RING_Z, *tile), BF16),
            pltpu.VMEM((RING_Y, *tile), BF16),
            pltpu.VMEM((RING_Y, *tile), BF16),
            pltpu.VMEM((RING_Z, *tile), BF16),
            pltpu.VMEM((RING_Y, *tile), BF16),
            pltpu.VMEM((RING_Z, *tile), BF16),
            pltpu.VMEM(ask, jnp.int32),
            pltpu.VMEM((RING_Y, *ask), jnp.int32),
            pltpu.VMEM((RING_Z, *ask), jnp.int32),
            pltpu.SMEM((RING_Y, *ask), jnp.int32),
            pltpu.SMEM((RING_Z, *ask), jnp.int32),
            dma((6,)),
            dma((2,)),
            dma((2,)),
            dma((6,)),
            dma((narrow_size,)),
            dma((6,)),
            dma((6,)),
            dma((narrow_size,)),
            dma((narrow_size,)),
            dma((14,)),
            dma((lists,)),
            dma((RING_Y,)),
            dma((RING_Z,)),
            dma((RING_Y,)),
            dma((RING_Z,)),
            dma((RING_Z,)),
            dma((RING_Z,)),
            dma((RING_Y,)),
            dma((RING_Y,)),
            dma((RING_Y,)),
            dma((RING_Y,)),
            dma((RING_Z,)),
            dma((RING_Z,)),
            dma((2,)),
            pltpu.SemaphoreType.REGULAR((4,)),
        ],
        compiler_params=pltpu.CompilerParams(
            collective_id=0, has_side_effects=True, vmem_limit_bytes=60 << 20
        ),
        name="rotate_lists",
    )(
        points.reshape(total, width),
        targets.reshape(total, width),
        centroids,
        block_list,
        lengths,
        sources,
    )
    return rotated.reshape(blocks, rows, width)


def solution(mesh):
    return jax.shard_map(
        local,
        mesh=mesh,
        in_specs=(
            P("wide", "narrow", None),
            P("wide", "narrow", None),
            P("wide", None),
            P("wide"),
            P("wide"),
            P("wide"),
        ),
        out_specs=P("wide", "narrow", None),
        check_vma=False,
    )
```

time: 72.5 us -> 62.1 us (0.86)
  Pallas kernels: 70.3 us -> 60 us
    pallas_call x2 -> x1, Pallas kernels: 70.3 us -> 60 us  [local(): pl.pallas_call(functools.partial(kernel, blocks, rows), out_shape=jax.Sha...]
where the time goes in v2:
time: 62.1 us; the launch traced here: 61.9 us
  Pallas kernels  60 us (97%)
  local copies, waits for them, and re-layouts  1.87 us (3%)
    pallas_call x1, Pallas kernels, local(): pl.pallas_call(functools.partial(kernel, blocks, rows), out_shape=jax.Sha...  60 us
    unnamed x1, local copies, waits for them, and re-layouts  1.87 us

profile of v2, /device:TPU:1, one launch (start us, length us, event | category | flops | bytes accessed | tf_op | source)
XLA Modules:
  0.0 61.9 jit_solution(9066575126566383346)
XLA Ops:
  0.0 60.0 %rotate_lists.1 = bf16[1024,256]{1,0:T(8,128)(2,1)} custom-call(bf16[1024,256]{1,0:T(8,128)(2,1)} %bitcast.4, bf16[1024,256]{1,0:T(8,128)(2,1)} %bitcast.5, f32[16,256]{1,0:T(8,128)} %centroids_hbm.1, s32[32]{0:T(128)} %block_list_hbm.1, s32[32]{0:T(128)} %lengths_hbm.1, s32[32]{0:T(128)} %sources_hbm.1), custom_call_target="tpu_custom_call" | custom-call | tf_op jit(solution)/shard_map/rotate_lists/pallas_call | solution.py:508
  60.0 1.9 %copy.8 = bf16[32,32,256]{2,1,0:T(8,128)(2,1)} copy(bf16[32,32,256]{2,1,0:T(8,128)(2,1)} %bitcast.3) | data formatting | bytes 1048576

commit v3 on v2

--- a/solution.py
+++ b/solution.py
@@ -81,7 +81,8 @@
     mine,
     rot,
     swap_out,
-    swap_in,
+    swap_in0,
+    swap_in1,
     hand0,
     hand1,
     got_z,
@@ -226,11 +227,36 @@
                 piece * width : (piece + 1) * width, :
             ].T
 
+    def half_gram(owner_chip, which, first, held):
+        wanted = (owner_chip * 2 + core) * PER_DEV + which
+        pieces = []
+        for b in range(blocks):
+            keep = jnp.where(block_list[b] == wanted, 1.0, 0.0).astype(BF16)
+            pieces.append(held[b * rows : (b + 1) * rows, :] * keep)
+        return mm(turned_t[:, first : first + total], jnp.concatenate(pieces, axis=0))
+
+    def own_half(owner_chip, which):
+        return half_gram(owner_chip, which, 0, res)
+
+    def sib_half(owner_chip, which):
+        return half_gram(owner_chip, which, total, res_sib)
+
+    def hop(slot, where):
+        return remote(
+            out_buf.at[slot], in_buf.at[slot], gram_send.at[slot], gram_recv.at[slot], {"narrow": where}
+        )
+
+    hops = [hop(s, right if s % 2 == 0 else left) for s in range(6)]
+    sent += hops
+    early = ((opposite, 0), (opposite, 1), (right_chip, 1), (left_chip, 0))
+
     loads[0].wait()
     transpose_into(0, own_t)
     for load in loads[1:]:
         load.wait()
     residual_into(res, own_p, narrow * rows)
+    for slot, (owner_chip, which) in enumerate(early):
+        kept[slot] = own_half(owner_chip, which)
     swap_t.wait_recv()
     transpose_into(total, sib_t)
     swap_p.wait_recv()
@@ -238,62 +264,46 @@
     share_raw(raw.at[left], left, right)
     residual_into(res_sib, sib_p, sibling * rows)
 
-    def gram(owner_chip, which):
-        wanted = (owner_chip * 2 + core) * PER_DEV + which
-        pieces = []
-        for held in (res, res_sib):
-            for b in range(blocks):
-                keep = jnp.where(block_list[b] == wanted, 1.0, 0.0).astype(BF16)
-                pieces.append(held[b * rows : (b + 1) * rows, :] * keep)
-        return mm(turned_t[...], jnp.concatenate(pieces, axis=0))
-
-    def hop(slot, where):
-        return remote(
-            out_buf.at[slot], in_buf.at[slot], gram_send.at[slot], gram_recv.at[slot], {"narrow": where}
-        )
-
-    hops = [hop(s, right if s % 2 == 0 else left) for s in range(6)]
-    sent += hops
-    out_buf[0] = gram(opposite, 0).astype(BF16)
-    hops[0].start()
-    out_buf[1] = gram(opposite, 1).astype(BF16)
-    hops[1].start()
+    def finish(slot):
+        owner_chip, which = early[slot]
+        out_buf[slot] = (kept[slot] + sib_half(owner_chip, which)).astype(BF16)
+        hops[slot].start()
+
+    finish(0)
+    finish(1)
     hear((0, 1, 2, 3))
     tell()
-    out_buf[2] = gram(right_chip, 1).astype(BF16)
-    hops[2].start()
+    finish(2)
     share_raw(raw.at[left], left, sibling)
     raw_arrived(right)
     share_raw(raw.at[right], right, sibling)
-    out_buf[3] = gram(left_chip, 0).astype(BF16)
-    hops[3].start()
+    finish(3)
     hear((0, 1, 2, 3))
     tell()
-    kept[0] = gram(right_chip, 0)
-    kept[1] = gram(left_chip, 1)
-    hear((0, 1, 2, 3))
-    tell_z()
-    across = opposite * 2 + core
-    raw_arrived(across)
-    share_raw(raw.at[across], across, sibling)
-    kept[2] = gram(chip, 0)
-    hear((2, 3))
-    tell_z()
-    kept[3] = gram(chip, 1)
-    hear((2, 3))
-
-    line = lax.broadcasted_iota(jnp.int32, ask.shape, 0)
-    wish = jnp.where(line == 0, sources[0], sources[1])
-    ask[...] = wish
-    ask_y[at_y] = wish
-    ask_z[at_z] = wish
-
+    kept[0] = own_half(right_chip, 0) + sib_half(right_chip, 0)
+    kept[1] = own_half(left_chip, 1) + sib_half(left_chip, 1)
     hops[0].wait_recv()
     out_buf[4] = (kept[0] + in_buf[0].astype(F32)).astype(BF16)
     hops[4].start()
     hops[1].wait_recv()
     out_buf[5] = (kept[1] + in_buf[1].astype(F32)).astype(BF16)
     hops[5].start()
+    hear((0, 1, 2, 3))
+    tell_z()
+    across = opposite * 2 + core
+    raw_arrived(across)
+    share_raw(raw.at[across], across, sibling)
+    kept[2] = own_half(chip, 0) + sib_half(chip, 0)
+    hear((2, 3))
+    tell_z()
+    kept[3] = own_half(chip, 1) + sib_half(chip, 1)
+    hear((2, 3))
+
+    line = lax.broadcasted_iota(jnp.int32, ask.shape, 0)
+    wish = jnp.where(line == 0, sources[0], sources[1])
+    ask[...] = wish
+    ask_y[at_y] = wish
+    ask_z[at_z] = wish
 
     for step in y_steps:
         other, where = y_peer(step)
@@ -351,22 +361,31 @@
         mine[which] = rotation
         rot[narrow * PER_DEV + which] = rotation
 
-    x_moves = []
+    swap_in = (swap_in0, swap_in1)
+    x_peers = []
+    for chip_step, flip in ((2, 0), (2, 1), (1, 0), (1, 1), (3, 0), (3, 1), (0, 1)):
+        peer_core = core + flip - 2 * core * flip
+        x_peers.append(((chip + chip_step) % CHIPS_X) * 2 + peer_core)
     for b in range(MOVE):
         chosen = mine[block_list[b] % PER_DEV]
-        swap_out[:, b * rows : (b + 1) * rows, :] = (
-            mm_nt(hand_res[b], chosen).astype(BF16).reshape(2 * CHIPS_X, rows, width)
-        )
-    swap_in[narrow] = swap_out[narrow]
-    for chip_step, flip in ((2, 0), (2, 1), (1, 0), (1, 1), (3, 0), (3, 1), (0, 1)):
-        peer_core = core + flip - 2 * core * flip
-        peer = ((chip + chip_step) % CHIPS_X) * 2 + peer_core
-        copy = remote(
-            swap_out.at[peer], swap_in.at[narrow], x_send.at[peer], x_recv.at[narrow], {"narrow": peer}
-        )
-        copy.start()
-        x_moves.append((copy, peer))
-    sent += [copy for copy, peer in x_moves]
+        swap_out[b] = mm_nt(hand_res[b], chosen).astype(BF16).reshape(2 * CHIPS_X, rows, width)
+        swap_in[b][narrow] = swap_out[b, narrow]
+        for peer in x_peers:
+            copy = remote(
+                swap_out.at[b, peer],
+                swap_in[b].at[narrow],
+                x_send.at[b, peer],
+                x_recv.at[b, narrow],
+                {"narrow": peer},
+            )
+            copy.start()
+            sent.append(copy)
+
+    def x_arrived(b):
+        for peer in x_peers:
+            remote(
+                swap_out.at[b, peer], swap_in[b].at[peer], x_send.at[b, peer], x_recv.at[b, peer], {"narrow": peer}
+            ).wait_recv()
 
     def place(owner_chip, owner_core, which):
         return (owner_chip * 2 + owner_core) * PER_DEV + which
@@ -383,9 +402,7 @@
     def arrived(slot):
         remote(rot.at[slot], rot.at[slot], rot_send.at[0], rot_recv.at[slot], {"narrow": sibling}).wait_recv()
 
-    share(place(chip, core, 0), right)
     share(place(chip, core, 1), left)
-    share(place(chip, core, 1), right)
     share(place(chip, core, 0), left)
     share(place(chip, core, 0), sibling)
     share(place(chip, core, 1), sibling)
@@ -403,26 +420,26 @@
     to_scalars_y.wait()
     to_scalars_z.wait()
 
-    for copy, peer in x_moves:
-        remote(
-            swap_out.at[peer], swap_in.at[peer], x_send.at[peer], x_recv.at[peer], {"narrow": peer}
-        ).wait_recv()
-    first = swap_in[block_list[0] // PER_DEV][0:rows, :]
-    second = swap_in[block_list[1] // PER_DEV][rows : 2 * rows, :]
+    x_arrived(0)
+    first = swap_in0[block_list[0] // PER_DEV]
     hand0[...] = first
+    got_z[at_z] = first
+    for step in z_steps:
+        other, where = z_peer(step)
+        copy = remote(hand0, got_z.at[at_z], g_sz.at[step], g_rz.at[at_z], where)
+        copy.start()
+        sent.append(copy)
+    share(place(chip, core, 0), right)
+    share(place(chip, core, 1), right)
+    x_arrived(1)
+    second = swap_in1[block_list[1] // PER_DEV]
     hand1[...] = second
-    got_z[at_z] = first
     got_y[at_y] = second
     for step in y_steps:
         other, where = y_peer(step)
         copy = remote(hand1, got_y.at[at_y], g_sy.at[step], g_ry.at[at_y], where)
         copy.start()
         sent.append(copy)
-    for step in z_steps:
-        other, where = z_peer(step)
-        copy = remote(hand0, got_z.at[at_z], g_sz.at[step], g_rz.at[at_z], where)
-        copy.start()
-        sent.append(copy)
 
     def turn(b):
         base = pl.multiple_of(b * rows, rows)
@@ -433,13 +450,6 @@
 
     def from_z(source):
         return source // blocks % RING_Z
-
-    arrived(place(right_chip, core, 1))
-    share(place(right_chip, core, 1), left)
-    share(place(right_chip, core, 1), sibling)
-    arrived(place(left_chip, core, 0))
-    share(place(left_chip, core, 0), right)
-    share(place(left_chip, core, 0), sibling)
 
     for step in y_steps:
         other, where = y_peer(step)
@@ -452,10 +462,12 @@
         copy.start()
         sent.append(copy)
 
-    arrived(place(right_chip, core, 0))
-    share(place(right_chip, core, 0), sibling)
-    arrived(place(left_chip, core, 1))
-    share(place(left_chip, core, 1), sibling)
+    arrived(place(right_chip, core, 1))
+    share(place(right_chip, core, 1), left)
+    share(place(right_chip, core, 1), sibling)
+    arrived(place(left_chip, core, 0))
+    share(place(left_chip, core, 0), right)
+    share(place(left_chip, core, 0), sibling)
 
     for step in z_steps:
         other, where = z_peer(step)
@@ -468,6 +480,10 @@
         copy.start()
         sent.append(copy)
 
+    arrived(place(right_chip, core, 0))
+    share(place(right_chip, core, 0), sibling)
+    arrived(place(left_chip, core, 1))
+    share(place(left_chip, core, 1), sibling)
     arrived(place(opposite, core, 1))
     share(place(opposite, core, 1), sibling)
     arrived(place(opposite, core, 0))
@@ -507,7 +523,7 @@
     ask = (8, 128)
     rotated = pl.pallas_call(
         functools.partial(kernel, blocks, rows),
-        out_shape=jax.ShapeDtypeStruct((total, width), BF16),
+        out_shape=pltpu.VMEM((total, width), BF16),
         in_specs=[hbm] * 6,
         out_specs=pl.BlockSpec(memory_space=pltpu.VMEM),
         scratch_shapes=[
@@ -525,8 +541,9 @@
             pltpu.VMEM((PER_DEV, *square), F32),
             pltpu.VMEM((PER_DEV, *square), BF16),
             pltpu.VMEM((lists, *square), BF16),
-            pltpu.VMEM((narrow_size, MOVE * rows, width), BF16),
-            pltpu.VMEM((narrow_size, MOVE * rows, width), BF16),
+            pltpu.VMEM((MOVE, narrow_size, rows, width), BF16),
+            pltpu.VMEM((narrow_size, rows, width), BF16),
+            pltpu.VMEM((narrow_size, rows, width), BF16),
             pltpu.VMEM(tile, BF16),
             pltpu.VMEM(tile, BF16),
             pltpu.VMEM((RING_Z, *tile), BF16),
@@ -547,8 +564,8 @@
             dma((narrow_size,)),
             dma((6,)),
             dma((6,)),
-            dma((narrow_size,)),
-            dma((narrow_size,)),
+            dma((MOVE, narrow_size)),
+            dma((MOVE, narrow_size)),
             dma((14,)),
             dma((lists,)),
             dma((RING_Y,)),

time: 62.1 us -> 59.6 us (0.960)
  Pallas kernels: 60 us -> 58.7 us
  local copies, waits for them, and re-layouts: 1.87 us -> 0.8 us
    pallas_call x1, Pallas kernels: 60 us -> 58.7 us  [local(): pl.pallas_call(functools.partial(kernel, blocks, rows), out_shape=pltpu.V...]
    unnamed x1, local copies, waits for them, and re-layouts: 1.87 us -> 0.8 us
where the time goes in v3:
time: 59.6 us; the launch traced here: 59.5 us
  Pallas kernels  58.7 us (98%)
  local copies, waits for them, and re-layouts  0.8 us (1%)
    pallas_call x1, Pallas kernels, local(): pl.pallas_call(functools.partial(kernel, blocks, rows), out_shape=pltpu.V...  58.7 us

profile of v3, /device:TPU:1, one launch (start us, length us, event | category | flops | bytes accessed | tf_op | source)
XLA Modules:
  0.0 59.5 jit_solution(16721051167941467968)
XLA Ops:
  0.0 58.7 %rotate_lists.1 = bf16[1024,256]{1,0:T(8,128)(2,1)S(1)} custom-call(bf16[1024,256]{1,0:T(8,128)(2,1)} %bitcast.4, bf16[1024,256]{1,0:T(8,128)(2,1)} %bitcast.5, f32[16,256]{1,0:T(8,128)} %centroids_hbm.1, s32[32]{0:T(128)} %block_list_hbm.1, s32[32]{0:T(128)} %lengths_hbm.1, s32[32]{0:T(128)} %sources_hbm.1), custom_call_target="tpu_custom_call" | custom-call | tf_op jit(solution)/shard_map/rotate_lists/pallas_call | solution.py:524
  58.7 0.8 %copy.8 = bf16[32,32,256]{2,1,0:T(8,128)(2,1)} copy(bf16[32,32,256]{2,1,0:T(8,128)(2,1)S(1)} %bitcast.3) | data formatting | bytes 1048576

commit v4 on v3

--- a/solution.py
+++ b/solution.py
@@ -13,6 +13,7 @@
 RING_Y = 8
 RING_Z = 12
 PER_DEV = 2
+REACH = 3
 
 MESH = pl.DeviceIdType.MESH
 BF16 = jnp.bfloat16
@@ -366,7 +367,7 @@
     for chip_step, flip in ((2, 0), (2, 1), (1, 0), (1, 1), (3, 0), (3, 1), (0, 1)):
         peer_core = core + flip - 2 * core * flip
         x_peers.append(((chip + chip_step) % CHIPS_X) * 2 + peer_core)
-    for b in range(MOVE):
+    for b in reversed(range(MOVE)):
         chosen = mine[block_list[b] % PER_DEV]
         swap_out[b] = mm_nt(hand_res[b], chosen).astype(BF16).reshape(2 * CHIPS_X, rows, width)
         swap_in[b][narrow] = swap_out[b, narrow]
@@ -420,17 +421,6 @@
     to_scalars_y.wait()
     to_scalars_z.wait()
 
-    x_arrived(0)
-    first = swap_in0[block_list[0] // PER_DEV]
-    hand0[...] = first
-    got_z[at_z] = first
-    for step in z_steps:
-        other, where = z_peer(step)
-        copy = remote(hand0, got_z.at[at_z], g_sz.at[step], g_rz.at[at_z], where)
-        copy.start()
-        sent.append(copy)
-    share(place(chip, core, 0), right)
-    share(place(chip, core, 1), right)
     x_arrived(1)
     second = swap_in1[block_list[1] // PER_DEV]
     hand1[...] = second
@@ -440,6 +430,56 @@
         copy = remote(hand1, got_y.at[at_y], g_sy.at[step], g_ry.at[at_y], where)
         copy.start()
         sent.append(copy)
+    share(place(chip, core, 0), right)
+    share(place(chip, core, 1), right)
+    x_arrived(0)
+    first = swap_in0[block_list[0] // PER_DEV]
+    hand0[...] = first
+    got_z[at_z] = first
+    for step in (REACH, RING_Z - REACH, 2, RING_Z - 2, 1, RING_Z - 1):
+        other, where = z_peer(step)
+        copy = remote(hand0, got_z.at[at_z], g_sz.at[step], g_rz.at[at_z], where)
+        copy.start()
+        sent.append(copy)
+
+    def z_arrived(step):
+        other, where = z_peer(step)
+        remote(hand0, got_z.at[other], g_sz.at[step], g_rz.at[other], where).wait_recv()
+
+    def z_relay(source_step, onward, index):
+        source, where = z_peer(source_step)
+        copy = remote(
+            got_z.at[source], got_z.at[source], g_sz.at[index], g_rz.at[source], z_peer(onward)[1]
+        )
+        copy.start()
+        sent.append(copy)
+
+    def share_if(here, slot, where, index):
+        copy = remote(
+            rot.at[slot], rot.at[slot], rot_send.at[index], rot_recv.at[slot], {"narrow": where}
+        )
+
+        @pl.when(here)
+        def _():
+            copy.start()
+
+        return copy
+
+    arrived(place(right_chip, core, 1))
+    share(place(right_chip, core, 1), left)
+    share(place(right_chip, core, 1), sibling)
+
+    z_arrived(RING_Z - REACH)
+    z_relay(RING_Z - REACH, 3, 6)
+    z_relay(RING_Z - REACH, 2, 5)
+    z_relay(RING_Z - REACH, 1, 4)
+    z_arrived(REACH)
+    z_relay(REACH, RING_Z - 2, 7)
+    z_relay(REACH, RING_Z - 1, 8)
+
+    arrived(place(left_chip, core, 0))
+    share_if(core == 0, place(left_chip, core, 0), right, 14)
+    share(place(left_chip, core, 0), sibling)
 
     def turn(b):
         base = pl.multiple_of(b * rows, rows)
@@ -462,16 +502,15 @@
         copy.start()
         sent.append(copy)
 
-    arrived(place(right_chip, core, 1))
-    share(place(right_chip, core, 1), left)
-    share(place(right_chip, core, 1), sibling)
-    arrived(place(left_chip, core, 0))
-    share(place(left_chip, core, 0), right)
-    share(place(left_chip, core, 0), sibling)
+    arrived(place(right_chip, core, 0))
+    odd_relay = share_if(core == 1, place(right_chip, core, 0), left, 14)
+    share(place(right_chip, core, 0), sibling)
+    arrived(place(left_chip, core, 1))
+    share(place(left_chip, core, 1), sibling)
 
     for step in z_steps:
-        other, where = z_peer(step)
-        remote(hand0, got_z.at[other], g_sz.at[step], g_rz.at[other], where).wait_recv()
+        if step not in (REACH, RING_Z - REACH):
+            z_arrived(step)
     last_y[at_y] = got_z[from_z(sources[0])]
     for step in y_steps:
         other, where = y_peer(step)
@@ -480,10 +519,6 @@
         copy.start()
         sent.append(copy)
 
-    arrived(place(right_chip, core, 0))
-    share(place(right_chip, core, 0), sibling)
-    arrived(place(left_chip, core, 1))
-    share(place(left_chip, core, 1), sibling)
     arrived(place(opposite, core, 1))
     share(place(opposite, core, 1), sibling)
     arrived(place(opposite, core, 0))
@@ -496,7 +531,7 @@
         out[pl.ds(pl.multiple_of(b * rows, rows), rows), :] = turn(b)
         return carry
 
-    lax.fori_loop(MOVE, blocks, turn_one, 0, unroll=2)
+    lax.fori_loop(MOVE, blocks, turn_one, 0, unroll=6)
 
     for step in y_steps:
         other, where = y_peer(step)
@@ -507,7 +542,7 @@
         remote(hand0, last_z.at[other], p_sz.at[step], p_rz.at[other], where).wait_recv()
     out[rows : 2 * rows, :] = last_z[from_z(sources[1])]
 
-    for copy in sent + raws + shares:
+    for copy in sent + raws + shares + [odd_relay]:
         copy.wait_send()
 
 
@@ -566,7 +601,7 @@
             dma((6,)),
             dma((MOVE, narrow_size)),
             dma((MOVE, narrow_size)),
-            dma((14,)),
+            dma((15,)),
             dma((lists,)),
             dma((RING_Y,)),
             dma((RING_Z,)),

time: 59.6 us -> 58.3 us (0.978)
  the two profiles are of different devices: /device:TPU:1 before, /device:TPU:2 now
where the time goes in v4:
time: 58.3 us; the launch traced here: 58.1 us
  Pallas kernels  57.3 us (98%)
  local copies, waits for them, and re-layouts  0.8 us (1%)
    pallas_call x1, Pallas kernels, local(): pl.pallas_call(functools.partial(kernel, blocks, rows), out_shape=pltpu.V...  57.3 us

profile of v4, /device:TPU:2, one launch (start us, length us, event | category | flops | bytes accessed | tf_op | source)
XLA Modules:
  0.0 58.1 jit_solution(12602287865034818087)
XLA Ops:
  0.0 57.3 %rotate_lists.1 = bf16[1024,256]{1,0:T(8,128)(2,1)S(1)} custom-call(bf16[1024,256]{1,0:T(8,128)(2,1)} %bitcast.4, bf16[1024,256]{1,0:T(8,128)(2,1)} %bitcast.5, f32[16,256]{1,0:T(8,128)} %centroids_hbm.1, s32[32]{0:T(128)} %block_list_hbm.1, s32[32]{0:T(128)} %lengths_hbm.1, s32[32]{0:T(128)} %sources_hbm.1), custom_call_target="tpu_custom_call" | custom-call | tf_op jit(solution)/shard_map/rotate_lists/pallas_call | solution.py:559
  57.4 0.8 %copy.8 = bf16[32,32,256]{2,1,0:T(8,128)(2,1)} copy(bf16[32,32,256]{2,1,0:T(8,128)(2,1)S(1)} %bitcast.3) | data formatting | bytes 1048576

commit v5 on v3

--- a/solution.py
+++ b/solution.py
@@ -341,7 +341,7 @@
     for which in range(PER_DEV):
         total_gram = kept[2 + which] + in_buf[4 + which].astype(F32)
         norm = jnp.sqrt(jnp.sum(total_gram * total_gram, keepdims=True) + 1e-06)
-        iterate[which] = total_gram / norm
+        iterate[which] = total_gram * (1.0 / norm)
 
     def sweep(index, carry):
         for which in range(PER_DEV):
@@ -441,6 +441,29 @@
         copy.start()
         sent.append(copy)
 
+    def z_arrived(step):
+        other, where = z_peer(step)
+        remote(hand0, got_z.at[other], g_sz.at[step], g_rz.at[other], where).wait_recv()
+
+    def share_if(here, slot, where, index):
+        copy = remote(
+            rot.at[slot], rot.at[slot], rot_send.at[index], rot_recv.at[slot], {"narrow": where}
+        )
+
+        @pl.when(here)
+        def _():
+            copy.start()
+
+        return copy
+
+    arrived(place(right_chip, core, 1))
+    share(place(right_chip, core, 1), left)
+    share(place(right_chip, core, 1), sibling)
+
+    arrived(place(left_chip, core, 0))
+    share_if(core == 0, place(left_chip, core, 0), right, 14)
+    share(place(left_chip, core, 0), sibling)
+
     def turn(b):
         base = pl.multiple_of(b * rows, rows)
         return mm_nt(res[pl.ds(base, rows), :], rot[block_list[b]]).astype(BF16)
@@ -462,16 +485,14 @@
         copy.start()
         sent.append(copy)
 
-    arrived(place(right_chip, core, 1))
-    share(place(right_chip, core, 1), left)
-    share(place(right_chip, core, 1), sibling)
-    arrived(place(left_chip, core, 0))
-    share(place(left_chip, core, 0), right)
-    share(place(left_chip, core, 0), sibling)
+    arrived(place(right_chip, core, 0))
+    odd_relay = share_if(core == 1, place(right_chip, core, 0), left, 14)
+    share(place(right_chip, core, 0), sibling)
+    arrived(place(left_chip, core, 1))
+    share(place(left_chip, core, 1), sibling)
 
     for step in z_steps:
-        other, where = z_peer(step)
-        remote(hand0, got_z.at[other], g_sz.at[step], g_rz.at[other], where).wait_recv()
+        z_arrived(step)
     last_y[at_y] = got_z[from_z(sources[0])]
     for step in y_steps:
         other, where = y_peer(step)
@@ -480,10 +501,6 @@
         copy.start()
         sent.append(copy)
 
-    arrived(place(right_chip, core, 0))
-    share(place(right_chip, core, 0), sibling)
-    arrived(place(left_chip, core, 1))
-    share(place(left_chip, core, 1), sibling)
     arrived(place(opposite, core, 1))
     share(place(opposite, core, 1), sibling)
     arrived(place(opposite, core, 0))
@@ -496,7 +513,7 @@
         out[pl.ds(pl.multiple_of(b * rows, rows), rows), :] = turn(b)
         return carry
 
-    lax.fori_loop(MOVE, blocks, turn_one, 0, unroll=2)
+    lax.fori_loop(MOVE, blocks, turn_one, 0, unroll=6)
 
     for step in y_steps:
         other, where = y_peer(step)
@@ -507,7 +524,7 @@
         remote(hand0, last_z.at[other], p_sz.at[step], p_rz.at[other], where).wait_recv()
     out[rows : 2 * rows, :] = last_z[from_z(sources[1])]
 
-    for copy in sent + raws + shares:
+    for copy in sent + raws + shares + [odd_relay]:
         copy.wait_send()
 
 
@@ -566,7 +583,7 @@
             dma((6,)),
             dma((MOVE, narrow_size)),
             dma((MOVE, narrow_size)),
-            dma((14,)),
+            dma((15,)),
             dma((lists,)),
             dma((RING_Y,)),
             dma((RING_Z,)),

time: 59.6 us -> 57.8 us (0.970)
  Pallas kernels: 58.7 us -> 56.6 us
    pallas_call x1, Pallas kernels: 58.7 us -> 56.6 us  [local(): pl.pallas_call(functools.partial(kernel, blocks, rows), out_shape=pltpu.V...]
where the time goes in v5:
time: 57.8 us; the launch traced here: 57.4 us
  Pallas kernels  56.6 us (98%)
  local copies, waits for them, and re-layouts  0.8 us (1%)
    pallas_call x1, Pallas kernels, local(): pl.pallas_call(functools.partial(kernel, blocks, rows), out_shape=pltpu.V...  56.6 us

profile of v5, /device:TPU:1, one launch (start us, length us, event | category | flops | bytes accessed | tf_op | source)
XLA Modules:
  0.0 57.4 jit_solution(13956102981806570759)
XLA Ops:
  0.0 56.6 %rotate_lists.1 = bf16[1024,256]{1,0:T(8,128)(2,1)S(1)} custom-call(bf16[1024,256]{1,0:T(8,128)(2,1)} %bitcast.4, bf16[1024,256]{1,0:T(8,128)(2,1)} %bitcast.5, f32[16,256]{1,0:T(8,128)} %centroids_hbm.1, s32[32]{0:T(128)} %block_list_hbm.1, s32[32]{0:T(128)} %lengths_hbm.1, s32[32]{0:T(128)} %sources_hbm.1), custom_call_target="tpu_custom_call" | custom-call | tf_op jit(solution)/shard_map/rotate_lists/pallas_call | solution.py:541
  56.6 0.8 %copy.8 = bf16[32,32,256]{2,1,0:T(8,128)(2,1)} copy(bf16[32,32,256]{2,1,0:T(8,128)(2,1)S(1)} %bitcast.3) | data formatting | bytes 1048576

commit v6 on v5

--- a/solution.py
+++ b/solution.py
@@ -463,6 +463,9 @@
     arrived(place(left_chip, core, 0))
     share_if(core == 0, place(left_chip, core, 0), right, 14)
     share(place(left_chip, core, 0), sibling)
+    arrived(place(right_chip, core, 0))
+    odd_relay = share_if(core == 1, place(right_chip, core, 0), left, 14)
+    share(place(right_chip, core, 0), sibling)
 
     def turn(b):
         base = pl.multiple_of(b * rows, rows)
@@ -485,12 +488,6 @@
         copy.start()
         sent.append(copy)
 
-    arrived(place(right_chip, core, 0))
-    odd_relay = share_if(core == 1, place(right_chip, core, 0), left, 14)
-    share(place(right_chip, core, 0), sibling)
-    arrived(place(left_chip, core, 1))
-    share(place(left_chip, core, 1), sibling)
-
     for step in z_steps:
         z_arrived(step)
     last_y[at_y] = got_z[from_z(sources[0])]
@@ -501,6 +498,8 @@
         copy.start()
         sent.append(copy)
 
+    arrived(place(left_chip, core, 1))
+    share(place(left_chip, core, 1), sibling)
     arrived(place(opposite, core, 1))
     share(place(opposite, core, 1), sibling)
     arrived(place(opposite, core, 0))

time: 57.8 us -> 57.8 us (level)
  no operation moved by 1% of the time
where the time goes in v6:
time: 57.8 us; the launch traced here: 57.4 us
  Pallas kernels  56.5 us (98%)
  local copies, waits for them, and re-layouts  0.8 us (1%)
    pallas_call x1, Pallas kernels, local(): pl.pallas_call(functools.partial(kernel, blocks, rows), out_shape=pltpu.V...  56.5 us

profile of v6, /device:TPU:1, one launch (start us, length us, event | category | flops | bytes accessed | tf_op | source)
XLA Modules:
  0.0 57.4 jit_solution(12473849943659371036)
XLA Ops:
  0.0 56.5 %rotate_lists.1 = bf16[1024,256]{1,0:T(8,128)(2,1)S(1)} custom-call(bf16[1024,256]{1,0:T(8,128)(2,1)} %bitcast.4, bf16[1024,256]{1,0:T(8,128)(2,1)} %bitcast.5, f32[16,256]{1,0:T(8,128)} %centroids_hbm.1, s32[32]{0:T(128)} %block_list_hbm.1, s32[32]{0:T(128)} %lengths_hbm.1, s32[32]{0:T(128)} %sources_hbm.1), custom_call_target="tpu_custom_call" | custom-call | tf_op jit(solution)/shard_map/rotate_lists/pallas_call | solution.py:540
  56.6 0.8 %copy.8 = bf16[32,32,256]{2,1,0:T(8,128)(2,1)} copy(bf16[32,32,256]{2,1,0:T(8,128)(2,1)S(1)} %bitcast.3) | data formatting | bytes 1048576
